TPU v7x, 256 devices: a whole 4x4x8 slice. The times are simulated.
256 devices in a mesh: cells: 64 (over x_lo, y, z), tracers: 4 (over x_hi, core).
Axes of the slice: x: 4 (x_hi: 2, x_lo: 2; x = x_hi * 2 + x_lo), y: 4, z: 8, core: 2. Of those that a mesh axis runs over, the one named last changes fastest.
Arguments:
- pulses: float32 [4096, 256, 128], P('tracers', 'cells'), may hold values from -6 to 6
- wind_x: float32 [256, 128], P('cells'), may hold values from -0.24 to 0.24
- wind_y: float32 [256, 128], P('cells'), may hold values from -0.24 to 0.24
- obs_tile: int32 [8192, 1], P('cells'), may hold values from 0 to 63; in each aligned block of 128 rows (0 to 127, 128 to 255, ...) at most 4 rows name the same one
- obs_weight: bfloat16 [8192, 512], P('cells'), may hold values from 0.099609375 to 10
- obs_precision: bfloat16 [8192], P('cells'), may hold values from 0.0029907227 to 0.099609375
Outputs:
- gram: float32 [4096, 4096], P('cells', 'tracers')
Inputs may be any that keep to these rules, and one draw needn't show every extreme that they name: `obs_tile`: among the rows of one index of cells no tile is named by more than 4 rows, a bound that some block reaches of them.
All inputs are finite; a program needn't handle non-finite values.
Results may differ from a plain program's by a relative error of at most 0.0031.
Values may be sent and summed in bfloat16 or wider, within the bound.
No kernel may reach another device: no remote copies, remote signals or barrier semaphores. Data moves between devices by JAX's collectives and lax.ppermute only.
A program may use at most 64 MiB of HBM per device.

v0:
```python
import jax
import jax.numpy as jnp
from jax import lax
from jax.sharding import PartitionSpec as P

STEPS = 3


def passed_along(value, axis, steps):
    count = lax.axis_size(axis)
    pairs = [(source, (source + steps) % count) for source in range(count)]
    return lax.ppermute(value, axis, pairs)


def extended_2(shard, sides, width):
    for axis, dim in sides:
        peers, length = (lax.axis_size(axis), shard.shape[dim])
        up = [(i, (i + 1) % peers) for i in range(peers)]
        down = [(j, i) for i, j in up]
        last = lax.slice_in_dim(shard, length - width, length, axis=dim)
        leading = lax.slice_in_dim(shard, 0, width, axis=dim)
        before = lax.ppermute(last, axis, up)
        after = lax.ppermute(leading, axis, down)
        shard = jnp.concatenate([before, shard, after], axis=dim)
    return shard


def advance(extended, along_x, along_y):
    inner_rows = extended[:, 1:-1]
    behind = jnp.roll(inner_rows, 1, axis=2)
    flux_x = jnp.maximum(along_x, 0.0) * behind + jnp.minimum(along_x, 0.0) * inner_rows
    flux_y = (
        jnp.maximum(along_y, 0.0) * extended[:, :-1] + jnp.minimum(along_y, 0.0) * extended[:, 1:]
    )
    return inner_rows + flux_x - jnp.roll(flux_x, -1, axis=2) + flux_y[:, :-1] - flux_y[:, 1:]


def on_device(pulses, wind_x, wind_y, obs_tile, obs_weight, obs_precision):
    tracer_field = pulses
    next_row = passed_along(wind_y[:1], "cells", -1)
    faces_y = jnp.concatenate([wind_y, next_row], axis=0)
    for index_step in range(STEPS):
        extended = extended_2(tracer_field, (("cells", 1),), 1)
        tracer_field = advance(extended, wind_x, faces_y)
    cell_count = lax.axis_size("cells")
    obs_local = obs_tile.shape[0]
    slot_cap = 2 * obs_local // cell_count
    tile_index = obs_tile[:, 0]
    tile_match = (tile_index[:, None] == jnp.arange(cell_count, dtype=jnp.int32)[None, :]).astype(
        jnp.int32
    )
    slot_rank = jnp.sum((jnp.cumsum(tile_match, axis=0) - 1) * tile_match, axis=1)
    slot_target = tile_index * slot_cap + slot_rank
    weights_wide = obs_weight.astype(jnp.float32)
    averaging = (weights_wide / jnp.sum(weights_wide, axis=1, keepdims=True)).astype(jnp.bfloat16)
    send_rows = (
        jnp.zeros((cell_count * slot_cap, obs_weight.shape[1]), jnp.bfloat16)
        .at[slot_target]
        .set(averaging)
    )
    send_rows = send_rows.reshape(cell_count, slot_cap, obs_weight.shape[1])
    send_precision = (
        jnp.zeros((cell_count * slot_cap,), jnp.bfloat16).at[slot_target].set(obs_precision)
    )
    send_precision = send_precision.reshape(cell_count, slot_cap)
    tracer_rows = tracer_field.shape[0]
    sampled = tracer_field.astype(jnp.bfloat16).reshape(tracer_rows, -1)
    rows_in = lax.all_to_all(send_rows, "cells", split_axis=0, concat_axis=0, tiled=True)
    weight_in = lax.all_to_all(send_precision, "cells", split_axis=0, concat_axis=0, tiled=True)
    rows_jac = jnp.einsum(
        "nct,kt->nck", rows_in, sampled, preferred_element_type=jnp.float32
    ).astype(jnp.bfloat16)
    weighted = (weight_in.astype(jnp.float32)[:, :, None] * rows_jac.astype(jnp.float32)).astype(
        jnp.bfloat16
    )
    jac_rows = rows_jac
    weighted_rows = weighted
    slot_total = jac_rows.shape[0] * jac_rows.shape[1]
    jac_rows = jac_rows.reshape(slot_total, tracer_rows)
    weighted_rows = weighted_rows.reshape(slot_total, tracer_rows)
    partial_gram = lax.dot_general(
        lax.all_gather(jac_rows, "tracers", axis=1, tiled=True),
        weighted_rows,
        (((0,), (0,)), ((), ())),
        preferred_element_type=jnp.float32,
    )
    gram = lax.psum_scatter(partial_gram, "cells", scatter_dimension=0, tiled=True)
    return gram


def solution(mesh):
    placed = (
        P("tracers", "cells", None),
        P("cells", None),
        P("cells", None),
        P("cells", None),
        P("cells", None),
        P("cells"),
    )
    return jax.shard_map(
        on_device, mesh=mesh, in_specs=placed, out_specs=P("cells", "tracers"), check_vma=False
    )
```

profile of v0, /device:TPU:4, one launch (start us, length us, event | category | flops | bytes accessed | tf_op | source)
XLA Modules:
  0.0 513.9 jit_solution(178086579286610043)
XLA Ops:
  6.5 0.7 slice.95
  7.2 8.9 %collective-permute-start = (f32[1,128]{1,0:T(1,128)S(1)}, f32[1,128]{1,0:T(1,128)S(1)}, u32[]{:S(2)}, u32[]{:S(2)}) collective-permute-start(f32[1,128]{1,0:T(1,128)S(1)} %slice.95), channel_id=1, source_target_pairs={{0,252},{4,0},{8,4},{12,8},{16,12},{20,16},{24,20},{28,24},{32,28}... | collective-permute-start | bytes 1544 | tf_op jit(solution)/shard_map/ppermute | solution.py:12
  16.2 3.9 fusion.21
  20.1 6.2 %collective-permute-start.2 = (f32[1024,1,128]{2,0,1:T(8,128)}, f32[1024,1,128]{2,0,1:T(8,128)}, u32[]{:S(2)}, u32[]{:S(2)}) collective-permute-start(f32[1024,1,128]{2,0,1:T(8,128)} %bitcast.8), channel_id=1, source_target_pairs={{4,0},{8,4},{12,8},{16,12},{20,16},{24,20},{28,24},{32,28},{36,32}... | collective-permute-start | bytes 1572872 | tf_op jit(solution)/shard_map/ppermute | solution.py:23
  26.3 1.9 copy.27
  28.3 0.4 fusion.4
  28.8 2.0 slice.118
  30.7 0.2 copy-done.2
  30.9 6.8 %collective-permute-done.1 = f32[1024,1,128]{2,0,1:T(8,128)S(1)} collective-permute-done((f32[1024,1,128]{2,0,1:T(8,128)S(1)}, f32[1024,1,128]{2,0,1:T(8,128)S(1)}, u32[]{:S(2)}, u32[]{:S(2)}) %collective-permute-start.1) | collective-permute-done | bytes 524320 | tf_op jit(solution)/shard_map/ppermute | solution.py:22
  37.7 0.2 copy.29
  37.9 1.2 copy.33
  39.2 0.4 fusion
  39.6 1.2 copy-done.3
  40.8 0.6 copy-done.8
  41.4 2.7 slice_subtract_fusion.2
  44.1 0.1 fusion.20
  44.2 1.3 copy.36
  45.4 0.2 copy.34
  45.6 0.1 collective-permute-start.3
  45.7 6.2 %collective-permute-start.4 = (f32[1024,1,128]{2,0,1:T(8,128)}, f32[1024,1,128]{2,0,1:T(8,128)}, u32[]{:S(2)}, u32[]{:S(2)}) collective-permute-start(f32[1024,1,128]{2,0,1:T(8,128)} %copy.36), channel_id=1, source_target_pairs={{4,0},{8,4},{12,8},{16,12},{20,16},{24,20},{28,24},{32,28},{36,32}... | collective-permute-start | bytes 1572872 | tf_op jit(solution)/shard_map/ppermute | solution.py:23
  52.0 0.1 fusion.13
  52.0 0.2 reduce_window_sum.11
  52.2 0.2 select_reduce_fusion
  52.4 0.4 fusion.5
  52.9 1.8 slice.124
  54.6 0.2 copy-done.6
  54.8 7.7 %collective-permute-done.3 = f32[1024,1,128]{2,0,1:T(8,128)} collective-permute-done((f32[1024,1,128]{2,0,1:T(8,128)S(1)}, f32[1024,1,128]{2,0,1:T(8,128)}, u32[]{:S(2)}, u32[]{:S(2)}) %collective-permute-start.3) | collective-permute-done | bytes 524320 | tf_op jit(solution)/shard_map/ppermute | solution.py:22
  62.6 1.2 copy.35
  63.8 1.2 copy.37
  65.1 0.4 fusion.1
  65.5 1.2 copy-done.7
  66.7 0.6 copy-done.10
  67.3 2.7 slice_subtract_fusion.1
  70.0 0.1 fusion.19
  70.1 1.0 copy.40
  71.1 0.2 copy.38
  71.3 0.1 collective-permute-start.5
  71.4 6.2 %collective-permute-start.6 = (f32[1024,1,128]{2,0,1:T(8,128)}, f32[1024,1,128]{2,0,1:T(8,128)}, u32[]{:S(2)}, u32[]{:S(2)}) collective-permute-start(f32[1024,1,128]{2,0,1:T(8,128)} %copy.40), channel_id=1, source_target_pairs={{4,0},{8,4},{12,8},{16,12},{20,16},{24,20},{28,24},{32,28},{36,32}... | collective-permute-start | bytes 1572872 | tf_op jit(solution)/shard_map/ppermute | solution.py:23
  77.6 1.5 scatter_custom_fusion.1
  79.1 0.7 all_to_all.12
  79.8 4.6 all-to-all-start.1
  84.4 0.1 convert_reduce_fusion
  84.5 1.2 scatter_custom_fusion
  85.7 0.8 reshape.57
  86.5 8.4 %all-to-all-done.1 = bf16[64,1,4]{2,1,0:T(2,128)(2,1)S(1)} async-done(((bf16[64,1,4]{2,1,0:T(2,128)(2,1)}), bf16[64,1,4]{2,1,0:T(2,128)(2,1)S(1)}, u32[]{:S(2)}, u32[]{:S(2)}) %all-to-all-start.1) | async-done | bytes 544 | tf_op jit(solution)/shard_map/all_to_all | solution.py:69
  94.9 4.6 all-to-all-start
  99.7 0.4 fusion.6
  100.2 1.7 slice.132
  101.9 0.2 copy-done.4
  102.1 1.2 copy.39
  103.4 1.2 copy.41
  104.7 0.4 fusion.2
  105.0 1.2 copy-done.5
  106.2 0.6 copy-done.9
  106.9 1.2 fusion.3
  108.0 3.6 all-to-all-done
  111.7 0.4 multiply_convert_fusion
  112.1 0.4 copy.44
  112.6 0.9 reshape.59
  113.6 0.4 copy.47
  114.0 0.1 reshape.60
  114.1 23.7 %all-gather.2.cloned.1.call-done = bf16[256,4096]{1,0:T(8,128)(2,1)} async-done(((bf16[256,1024]{1,0:T(8,128)(2,1)}), bf16[256,4096]{1,0:T(8,128)(2,1)}) %all-gather.2.cloned.1.call-update) | async-done | bytes 2097168 | tf_op jit(solution)/shard_map/all_gather | solution.py:82
  137.8 9.7 %fusion.22 = f32[4096,1024]{1,0:T(8,128)} fusion(bf16[256,4096]{1,0:T(8,128)(2,1)} %all-gather.2.cloned.1.call-done, bf16[256,1024]{1,0:T(8,128)(2,1)S(1)} %reshape.60), kind=kOutput, calls=%fused_computation.52 | convolution fusion | flops 2147483648 | bytes 19398656 | tf_op jit(solution)/shard_map/dot_general | solution.py:81
  147.5 359.5 %reduce-scatter.2.cloned.1.call-done = f32[64,1024]{1,0:T(8,128)} async-done(((f32[4096,1024]{1,0:T(8,128)}), f32[64,1024]{1,0:T(8,128)}) %reduce-scatter.2.cloned.1.call-update) | async-done | bytes 262160 | tf_op jit(solution)/shard_map/reduce_scatter | solution.py:87
  (42 shorter events, 0.4 us)
Async XLA Ops:
  6.5 19.8 %copy-start.13 = (f32[4,128]{1,0:T(4,128)S(1)}, f32[4,128]{1,0:T(4,128)}, u32[]{:S(2)}) copy-start(f32[4,128]{1,0:T(4,128)} %param.7) | copy-start | bytes 6148
  7.2 23.7 %collective-permute-start = (f32[1,128]{1,0:T(1,128)S(1)}, f32[1,128]{1,0:T(1,128)S(1)}, u32[]{:S(2)}, u32[]{:S(2)}) collective-permute-start(f32[1,128]{1,0:T(1,128)S(1)} %slice.95), channel_id=1, source_target_pairs={{0,252},{4,0},{8,4},{12,8},{16,12},{20,16},{24,20},{28,24},{32,28}... | collective-permute-start | bytes 1544 | tf_op jit(solution)/shard_map/ppermute | solution.py:12
  20.1 17.6 %collective-permute-start.1 = (f32[1024,1,128]{2,0,1:T(8,128)S(1)}, f32[1024,1,128]{2,0,1:T(8,128)S(1)}, u32[]{:S(2)}, u32[]{:S(2)}) collective-permute-start(f32[1024,1,128]{2,0,1:T(8,128)S(1)} %bitcast.25), channel_id=1, source_target_pairs={{0,4},{4,8},{8,12},{12,16},{16,20},{20,24},{24,28},{28,32},{32,36}... | collective-permute-start | bytes 1572872 | tf_op jit(solution)/shard_map/ppermute | solution.py:22
  20.1 17.8 %collective-permute-start.2 = (f32[1024,1,128]{2,0,1:T(8,128)}, f32[1024,1,128]{2,0,1:T(8,128)}, u32[]{:S(2)}, u32[]{:S(2)}) collective-permute-start(f32[1024,1,128]{2,0,1:T(8,128)} %bitcast.8), channel_id=1, source_target_pairs={{4,0},{8,4},{12,8},{16,12},{20,16},{24,20},{28,24},{32,28},{36,32}... | collective-permute-start | bytes 1572872 | tf_op jit(solution)/shard_map/ppermute | solution.py:23
  28.3 10.9 %copy-start.1 = (f32[1024,4,128]{0,2,1:T(8,128)}, f32[1024,4,128]{0,2,1:T(8,128)S(1)}, u32[]{:S(2)}) copy-start(f32[1024,4,128]{0,2,1:T(8,128)S(1)} %copy.27) | copy-start | bytes 6291460
  28.7 2.2 copy-start.2
  28.8 2.2 copy-start.14
  39.2 1.6 copy-start.3
  39.2 2.2 copy-start.8
  44.0 21.0 %copy-start = (f32[1024,4,128]{0,2,1:T(8,128)}, f32[1024,4,128]{0,2,1:T(8,128)S(1)}, u32[]{:S(2)}) copy-start(f32[1024,4,128]{0,2,1:T(8,128)S(1)} %slice_subtract_fusion.2) | copy-start | bytes 6291460
  44.1 7.9 %copy-start.12 = (s32[128,1]{0,1:T(1,128)S(1)}, s32[128,1]{0,1:T(1,128)}, u32[]{:S(2)}) copy-start(s32[128,1]{0,1:T(1,128)} %param.9) | copy-start | bytes 1540
  45.6 16.9 %collective-permute-start.3 = (f32[1024,1,128]{2,0,1:T(8,128)S(1)}, f32[1024,1,128]{2,0,1:T(8,128)}, u32[]{:S(2)}, u32[]{:S(2)}) collective-permute-start(f32[1024,1,128]{2,0,1:T(8,128)S(1)} %copy.34), channel_id=1, source_target_pairs={{0,4},{4,8},{8,12},{12,16},{16,20},{20,24},{24,28},{28,32},{32,36}... | collective-permute-start | bytes 1572872 | tf_op jit(solution)/shard_map/ppermute | solution.py:22
  45.7 18.1 %collective-permute-start.4 = (f32[1024,1,128]{2,0,1:T(8,128)}, f32[1024,1,128]{2,0,1:T(8,128)}, u32[]{:S(2)}, u32[]{:S(2)}) collective-permute-start(f32[1024,1,128]{2,0,1:T(8,128)} %copy.36), channel_id=1, source_target_pairs={{4,0},{8,4},{12,8},{16,12},{20,16},{24,20},{28,24},{32,28},{36,32}... | collective-permute-start | bytes 1572872 | tf_op jit(solution)/shard_map/ppermute | solution.py:23
  52.8 2.0 copy-start.6
  65.1 1.6 copy-start.7
  65.1 2.2 copy-start.10
  69.9 14.5 %copy-start.11 = (bf16[128,512]{1,0:T(8,128)(2,1)S(1)}, bf16[128,512]{1,0:T(8,128)(2,1)}, u32[]{:S(2)}) copy-start(bf16[128,512]{1,0:T(8,128)(2,1)} %param.10) | copy-start | bytes 393220
  71.3 30.9 %collective-permute-start.5 = (f32[1024,1,128]{2,0,1:T(8,128)S(1)}, f32[1024,1,128]{2,0,1:T(8,128)}, u32[]{:S(2)}, u32[]{:S(2)}) collective-permute-start(f32[1024,1,128]{2,0,1:T(8,128)S(1)} %copy.38), channel_id=1, source_target_pairs={{0,4},{4,8},{8,12},{12,16},{16,20},{20,24},{24,28},{28,32},{32,36}... | collective-permute-start | bytes 1572872 | tf_op jit(solution)/shard_map/ppermute | solution.py:22
  71.4 32.0 %collective-permute-start.6 = (f32[1024,1,128]{2,0,1:T(8,128)}, f32[1024,1,128]{2,0,1:T(8,128)}, u32[]{:S(2)}, u32[]{:S(2)}) collective-permute-start(f32[1024,1,128]{2,0,1:T(8,128)} %copy.40), channel_id=1, source_target_pairs={{4,0},{8,4},{12,8},{16,12},{20,16},{24,20},{28,24},{32,28},{36,32}... | collective-permute-start | bytes 1572872 | tf_op jit(solution)/shard_map/ppermute | solution.py:23
  79.8 15.1 %all-to-all-start.1 = ((bf16[64,1,4]{2,1,0:T(2,128)(2,1)}), bf16[64,1,4]{2,1,0:T(2,128)(2,1)S(1)}, u32[]{:S(2)}, u32[]{:S(2)}) async-start(bf16[64,1,4]{2,1,0:T(2,128)(2,1)} %all_to_all.12), calls=%async_computation.1 | async-start | bytes 65536 | tf_op jit(solution)/shard_map/all_to_all | solution.py:69
  94.9 16.8 %all-to-all-start = ((bf16[64,4,512]{2,1,0:T(4,128)(2,1)}), bf16[64,4,512]{2,1,0:T(4,128)(2,1)S(1)}, u32[]{:S(2)}, u32[]{:S(2)}) async-start(bf16[64,4,512]{2,1,0:T(4,128)(2,1)} %reshape.57), calls=%async_computation | async-start | bytes 524288 | tf_op jit(solution)/shard_map/all_to_all | solution.py:68
  99.5 38.2 %all-gather.2.cloned.1.call-start = ((), (), s32[]{:S(2)}) async-start(), calls=%async_computation.3 | async-start | bytes 2621440 | tf_op jit(solution)/shard_map/all_gather | solution.py:82
  100.1 2.0 copy-start.4
  104.6 1.6 copy-start.5
  104.6 2.2 copy-start.9
  113.5 393.5 %reduce-scatter.2.cloned.1.call-start = ((), (), s32[]{:S(2)}) async-start(), calls=%async_computation.4 | async-start | bytes 17039360 | tf_op jit(solution)/shard_map/reduce_scatter | solution.py:87
Sparse Core Ops, SparseCore 0:
  113.6 24.0 all-gather.1
  147.6 359.3 reduce-scatter.1
where the time goes:
time: 514 us
  waiting for transfers between devices  410 us (80%)
  starting transfers between devices  37.1 us (7%)
  local copies, waits for them, and re-layouts  32.4 us (6%)
  between operations  13.9 us (3%)
  other arithmetic  10.6 us (2%)
  matrix products  10.1 us (2%)
    reduce_scatter x1, waiting for transfers between devices, on_device(): lax.psum_scatter(partial_gram, 'cells', scatter_dimension=0, tiled=True)  360 us
    all_gather x1, waiting for transfers between devices, on_device(): lax.all_gather(jac_rows, 'tracers', axis=1, tiled=True)  23.7 us
    ppermute x3, starting transfers between devices, extended_2(): after = lax.ppermute(leading, axis, down)  18.7 us
    ppermute x3, waiting for transfers between devices, extended_2(): before = lax.ppermute(last, axis, up)  14.5 us
  transfers between devices with their start and end apart: 11, of which 6 were waited for; matrix products, arithmetic and copies ran while one was open for 4% of the time, Pallas kernels for 0%

commit v1 on v0

v1 whole, which is shorter than its diff:
```python
import jax
import jax.numpy as jnp
from jax import lax
from jax.experimental import pallas as pl
from jax.experimental.pallas import tpu as pltpu
from jax.sharding import Mesh, PartitionSpec as P

STEPS = 3
CAP = 4
XY = ("xl", "y")
CELLS = ("xl", "y", "z")
TRACERS = ("xh", "core")


def shifted(value, axis, steps):
    count = lax.axis_size(axis)
    return lax.ppermute(value, axis, [(i, (i + steps) % count) for i in range(count)])


def exchanged(value, axis):
    return lax.all_to_all(value, axis, split_axis=0, concat_axis=0, tiled=True)


def edge_rows(pulse_ref, first_ref, last_ref):
    count = first_ref.shape[1]
    rows = [pulse_ref[pl.ds(r, count, 4), :].astype(jnp.bfloat16) for r in range(4)]
    for r in range(STEPS):
        first_ref[r] = rows[r]
        last_ref[r] = rows[r + 1]


def edges(pulses, block=256):
    tracers = pulses.shape[0] // 4
    half = pl.BlockSpec((STEPS, block, 128), lambda i: (0, i, 0))
    shape = jax.ShapeDtypeStruct((STEPS, tracers, 128), jnp.bfloat16)
    return pl.pallas_call(
        edge_rows,
        grid=(tracers // block,),
        in_specs=[pl.BlockSpec((4 * block, 128), lambda i: (i, 0))],
        out_specs=[half, half],
        out_shape=[shape, shape],
        name="edges",
    )(pulses)


def jacobian_body(pulse_ref, above_ref, below_ref, wind_x_ref, wind_y_ref, rows_ref, out_ref):
    count = out_ref.shape[1]
    field = (
        [above_ref[r].astype(jnp.float32) for r in range(STEPS)]
        + [pulse_ref[pl.ds(r, count, 4), :] for r in range(4)]
        + [below_ref[r].astype(jnp.float32) for r in range(STEPS)]
    )
    wind_x = wind_x_ref[...]
    wind_y = wind_y_ref[...]
    gain_x, loss_x = jnp.maximum(wind_x, 0.0), jnp.minimum(wind_x, 0.0)
    gain_y, loss_y = jnp.maximum(wind_y, 0.0), jnp.minimum(wind_y, 0.0)
    from_right = -pltpu.roll(loss_x, 127, 1)
    keep_x = 1.0 + loss_x - pltpu.roll(gain_x, 127, 1)
    first = 1
    for step in range(STEPS):
        new = []
        for i in range(len(field) - 2):
            w = first + i - 1
            here = field[i + 1]
            keep = keep_x[w : w + 1] + loss_y[w : w + 1] - gain_y[w + 1 : w + 2]
            new.append(
                keep * here
                + gain_x[w : w + 1] * pltpu.roll(here, 1, 1)
                + from_right[w : w + 1] * pltpu.roll(here, 127, 1)
                + gain_y[w : w + 1] * field[i]
                - loss_y[w + 1 : w + 2] * field[i + 2]
            )
        field = new
        first += 1
    sampled = jnp.concatenate([f.astype(jnp.bfloat16) for f in field], axis=1)
    out_ref[...] = lax.dot_general(
        rows_ref[...], sampled, (((1,), (1,)), ((), ())), preferred_element_type=jnp.float32
    ).astype(jnp.bfloat16)


def jacobian(pulses, above, below, wind_x, wind_y, rows, block=128):
    tracers = pulses.shape[0] // 4
    slots = rows.shape[0]
    halo = pl.BlockSpec((STEPS, block, 128), lambda i: (0, i, 0))
    return pl.pallas_call(
        jacobian_body,
        grid=(tracers // block,),
        in_specs=[
            pl.BlockSpec((4 * block, 128), lambda i: (i, 0)),
            halo,
            halo,
            pl.BlockSpec((8, 128), lambda i: (0, 0)),
            pl.BlockSpec((16, 128), lambda i: (0, 0)),
            pl.BlockSpec((slots, 512), lambda i: (0, 0)),
        ],
        out_specs=pl.BlockSpec((slots, block), lambda i: (0, i)),
        out_shape=jax.ShapeDtypeStruct((slots, tracers), jnp.bfloat16),
        name="jacobian",
    )(pulses, above, below, wind_x, wind_y, rows)


def on_device(pulses, wind_x, wind_y, obs_tile, obs_weight, obs_precision):
    tracers = pulses.shape[0]
    cells = lax.axis_size(CELLS)
    obs = obs_tile.shape[0]
    pulses = pulses.reshape(tracers * 4, 128)

    first, last = edges(pulses)
    winds = jnp.concatenate([wind_x, wind_y], axis=0)
    above = shifted(last, CELLS, 1)
    below = shifted(first, CELLS, -1)
    winds_above = shifted(winds, CELLS, 1)
    winds_below = shifted(winds, CELLS, -1)
    wide_x = jnp.concatenate([winds_above[2:4], wind_x, winds_below[0:2]], axis=0)
    wide_y = jnp.concatenate(
        [winds_above[6:8], wind_y, winds_below[4:7], jnp.zeros((7, 128), jnp.float32)], axis=0
    )

    tile = obs_tile[:, 0]
    order = jnp.arange(obs)
    earlier = (tile[:, None] == tile[None, :]) & (order[None, :] < order[:, None])
    slot = tile * CAP + jnp.sum(earlier.astype(jnp.int32), axis=1)
    chosen = (slot[:, None] == jnp.arange(cells * CAP)[None, :]).astype(jnp.bfloat16)
    wide = obs_weight.astype(jnp.float32)
    averaging = (wide / jnp.sum(wide, axis=1, keepdims=True)).astype(jnp.bfloat16)
    rows_out = lax.dot_general(
        chosen, averaging, (((0,), (0,)), ((), ())), preferred_element_type=jnp.float32
    ).astype(jnp.bfloat16)
    rows_in = exchanged(rows_out.reshape(cells, CAP, 512), CELLS).reshape(cells * CAP, 512)

    jac_tile = jacobian(pulses, above, below, wide_x, wide_y, rows_in)
    jac_back = exchanged(jac_tile.reshape(cells, CAP, tracers), CELLS)
    jac = lax.dot_general(
        chosen,
        jac_back.reshape(cells * CAP, tracers),
        (((1,), (0,)), ((), ())),
        preferred_element_type=jnp.float32,
    )
    weighted = (obs_precision.astype(jnp.float32)[:, None] * jac).astype(jnp.bfloat16)
    jac = jac.astype(jnp.bfloat16)

    group = lax.axis_size(XY)
    cols = exchanged(jnp.broadcast_to(weighted, (group,) + weighted.shape), XY)
    both = exchanged(jnp.broadcast_to(jac, (2,) + jac.shape), "xh")
    four = exchanged(jnp.broadcast_to(both, (2,) + both.shape), "core").reshape(2, 2, obs, tracers)
    blocks = four.reshape(2, 2, obs, 2, tracers // 2).transpose(1, 0, 3, 2, 4)
    rows = exchanged(blocks.reshape(group, obs, tracers // 2), XY)

    partial = lax.dot_general(
        rows.reshape(group * obs, tracers // 2),
        cols.reshape(group * obs, tracers),
        (((0,), (0,)), ((), ())),
        preferred_element_type=jnp.float32,
    ).astype(jnp.bfloat16)
    depth = lax.axis_size("z")
    parts = exchanged(partial.reshape(depth, tracers // 2 // depth, tracers), "z")
    return jnp.sum(parts.astype(jnp.float32), axis=0)


def solution(mesh):
    fine = Mesh(mesh.devices.reshape(2, 4, 8, 2, 2), CELLS + TRACERS)
    placed = (
        P(TRACERS, CELLS, None),
        P(CELLS, None),
        P(CELLS, None),
        P(CELLS, None),
        P(CELLS, None),
        P(CELLS),
    )
    return jax.shard_map(
        on_device, mesh=fine, in_specs=placed, out_specs=P(CELLS, TRACERS), check_vma=False
    )
```

time: 514 us -> 182 us (0.35)
  waiting for transfers between devices: 410 us -> 32.8 us
  blocking collectives: 0 us -> 92.3 us
  local copies, waits for them, and re-layouts: 32.4 us -> 6.26 us
  between operations: 13.9 us -> 0.17 us
  Pallas kernels: 0 us -> 13 us
  matrix products: 10.1 us -> 1.86 us
  starting transfers between devices: 37.1 us -> 29.2 us
  other arithmetic: 10.6 us -> 3.16 us
    reduce_scatter x1 -> x0, waiting for transfers between devices: 360 us -> none  [on_device(): lax.psum_scatter(partial_gram, 'cells', scatter_dimension=0, tiled=True)]
    all_to_all x0 -> x5, blocking collectives: none -> 92.3 us  [exchanged(): return lax.all_to_all(value, axis, split_axis=0, concat_axis=0, tiled=True)]
    all_gather x1 -> x0, waiting for transfers between devices: 23.7 us -> none  [on_device(): lax.all_gather(jac_rows, 'tracers', axis=1, tiled=True)]
    all_to_all x2, waiting for transfers between devices: 12 us -> 32.7 us  [exchanged(): return lax.all_to_all(value, axis, split_axis=0, concat_axis=0, tiled=True)]
    ppermute x7 -> x4, waiting for transfers between devices: 14.5 us -> 0.01 us  [shifted(): lax.ppermute(value, axis, [(i, (i + steps) % count) for i in range(count)])]
    pallas_call x0 -> x2, Pallas kernels: none -> 13 us  [the longest x1 9.32 us: jacobian(): pl.pallas_call(jacobian_body, grid=(tracers // block,), in_specs=[pl.Bloc...]
    slice x17 -> x3, local copies, waits for them, and re-layouts: 13 us -> 0.01 us  [the longest x1 0.01 us: on_device(): winds_above[6:8]]
    ppermute x7 -> x4, starting transfers between devices: 27.8 us -> 15.2 us  [shifted(): lax.ppermute(value, axis, [(i, (i + steps) % count) for i in range(count)])]
  transfers between devices with their start and end apart: 11 -> 6, of which waited for: 6 -> 2; matrix products, arithmetic and copies ran while one was open for 4% -> 2% of each run, Pallas kernels for 0% -> 2%
where the time goes in v1:
time: 182 us; the launch traced here: 179 us
  blocking collectives  92.3 us (51%)
  waiting for transfers between devices  32.8 us (18%)
  starting transfers between devices  29.2 us (16%)
  Pallas kernels  13 us (7%)
  local copies, waits for them, and re-layouts  6.26 us (3%)
  other arithmetic  3.16 us (2%)
  matrix products  1.86 us (1%)
    all_to_all x5, blocking collectives, exchanged(): return lax.all_to_all(value, axis, split_axis=0, concat_axis=0, tiled=True)  92.3 us
    all_to_all x2, waiting for transfers between devices, exchanged(): return lax.all_to_all(value, axis, split_axis=0, concat_axis=0, tiled=True)  32.7 us
    ppermute x4, starting transfers between devices, shifted(): lax.ppermute(value, axis, [(i, (i + steps) % count) for i in range(count)])  15.2 us
    all_to_all x2, starting transfers between devices, exchanged(): return lax.all_to_all(value, axis, split_axis=0, concat_axis=0, tiled=True)  14 us
    pallas_call x1, Pallas kernels, jacobian(): pl.pallas_call(jacobian_body, grid=(tracers // block,), in_specs=[pl.Bloc...  9.32 us
    pallas_call x1, Pallas kernels, edges(): pl.pallas_call(edge_rows, grid=(tracers // block,), in_specs=[pl.BlockSpe...  3.7 us
  transfers between devices with their start and end apart: 6, of which 2 were waited for; matrix products, arithmetic and copies ran while one was open for 2% of the time, Pallas kernels for 2%

profile of v1, /device:TPU:4, one launch (start us, length us, event | category | flops | bytes accessed | tf_op | source)
XLA Modules:
  0.0 178.7 jit_solution(8134772992014681697)
XLA Ops:
  0.0 0.0 copy-start.5
  0.0 0.0 copy-start.2
  0.0 0.7 pad_maximum_fusion
  0.7 8.9 %collective-permute-start.3 = (f32[8,128]{1,0:T(8,128)S(1)}, f32[8,128]{1,0:T(8,128)S(1)}, u32[]{:S(2)}, u32[]{:S(2)}) collective-permute-start(f32[8,128]{1,0:T(8,128)S(1)} %pad_maximum_fusion), channel_id=1, source_target_pairs={{0,252},{4,0},{8,4},{12,8},{16,12},{20,16},{24,20},{28,24},{32,28}... | collective-permute-start | bytes 12296 | tf_op jit(solution)/shard_map/ppermute | solution.py:17
  9.7 0.0 collective-permute-start.2
  9.7 0.0 copy-start.4
  9.7 0.0 copy-start.3
  9.7 3.7 %edges.1 = (bf16[3,1024,128]{2,1,0:T(8,128)(2,1)}, bf16[3,1024,128]{2,1,0:T(8,128)(2,1)}) custom-call(f32[4096,128]{1,0:T(8,128)} %bitcast.18), custom_call_target="tpu_custom_call" | custom-call | tf_op jit(solution)/shard_map/edges/pallas_call | solution.py:36
  13.4 0.0 collective-permute-start
  13.4 6.2 %collective-permute-start.1 = (bf16[3,1024,128]{2,1,0:T(8,128)(2,1)}, bf16[3,1024,128]{2,1,0:T(8,128)(2,1)S(1)}, u32[]{:S(2)}, u32[]{:S(2)}) collective-permute-start(bf16[3,1024,128]{2,1,0:T(8,128)(2,1)} %get-tuple-element.8), channel_id=1, source_target_pairs={{0,252},{4,0},{8,4},{12,8},{16,12},{20,16},{24,20},{28,24},{32,28}... | collective-permute-start | bytes 2359304 | tf_op jit(solution)/shard_map/ppermute | solution.py:17
  19.6 0.0 copy-done.5
  19.6 0.2 convert_reduce_fusion.2
  19.8 0.0 copy-done.2
  19.8 0.1 convert_reduce_fusion.1
  20.0 0.3 convolution_convert_fusion
  20.3 0.8 reshape.31
  21.1 4.6 %all-to-all-start = ((bf16[64,4,512]{2,1,0:T(4,128)(2,1)}), bf16[64,4,512]{2,1,0:T(4,128)(2,1)S(1)}, u32[]{:S(2)}, u32[]{:S(2)}) async-start(bf16[64,4,512]{2,1,0:T(4,128)(2,1)} %reshape.31), calls=%async_computation | async-start | bytes 524288 | tf_op jit(solution)/shard_map/all_to_all | solution.py:21
  25.7 0.1 pad.3.clone
  25.8 0.0 collective-permute-done.3
  25.8 0.0 collective-permute-done.2
  25.8 0.0 copy-done.4
  25.8 0.6 pad_maximum_fusion.1.wind_x_ref
  26.4 0.0 copy-done.3
  26.4 0.7 maximum_maximum_fusion.wind_y_ref
  27.1 16.0 %all-to-all-done = bf16[64,4,512]{2,1,0:T(4,128)(2,1)S(1)} async-done(((bf16[64,4,512]{2,1,0:T(4,128)(2,1)}), bf16[64,4,512]{2,1,0:T(4,128)(2,1)S(1)}, u32[]{:S(2)}, u32[]{:S(2)}) %all-to-all-start) | async-done | bytes 262176 | tf_op jit(solution)/shard_map/all_to_all | solution.py:21
  43.1 0.8 reshape.32.rows_ref
  43.9 0.0 collective-permute-done.above_ref
  43.9 0.0 copy-start
  43.9 0.0 collective-permute-done.1.below_ref
  43.9 0.9 copy-done
  44.8 0.0 copy-start.1
  44.8 0.9 copy-done.1
  45.7 9.3 %jacobian.1 = bf16[256,1024]{1,0:T(8,128)(2,1)} custom-call(f32[4096,128]{1,0:T(8,128)} %bitcast.19, bf16[3,1024,128]{2,1,0:T(8,128)(2,1)} %copy-done, bf16[3,1024,128]{2,1,0:T(8,128)(2,1)} %copy-done.1, f32[8,128]{1,0:T(8,128)} %pad_maximum_fusion.1.wind_x_ref, f32[16,128]{1,0:T(8,128)} %maximum_maximum_fusion.wind_y_ref, bf16[256,512]{1,0:T(8,128)(2,1)} %reshape.32.rows_ref), custom_call_target="tpu_custom_call" | custom-call | tf_op jit(solution)/shard_map/jacobian/pallas_call | solution.py:85
  55.0 0.0 copy-start.6
  55.0 2.0 %reshape.33 = bf16[64,4,1024]{2,1,0:T(4,128)(2,1)} reshape(bf16[256,1024]{1,0:T(8,128)(2,1)} %jacobian.1) | data formatting | bytes 1048576 | tf_op jit(solution)/shard_map/reshape | solution.py:132
  57.1 9.4 %all-to-all-start.1 = ((bf16[64,4,1024]{2,1,0:T(4,128)(2,1)}), bf16[64,4,1024]{2,1,0:T(4,128)(2,1)S(1)}, u32[]{:S(2)}, u32[]{:S(2)}) async-start(bf16[64,4,1024]{2,1,0:T(4,128)(2,1)} %reshape.33), calls=%async_computation.1 | async-start | bytes 1048576 | tf_op jit(solution)/shard_map/all_to_all | solution.py:21
  66.5 0.0 copy-done.6
  66.5 16.7 %all-to-all-done.1 = bf16[64,4,1024]{2,1,0:T(4,128)(2,1)S(1)} async-done(((bf16[64,4,1024]{2,1,0:T(4,128)(2,1)}), bf16[64,4,1024]{2,1,0:T(4,128)(2,1)S(1)}, u32[]{:S(2)}, u32[]{:S(2)}) %all-to-all-start.1) | async-done | bytes 524320 | tf_op jit(solution)/shard_map/all_to_all | solution.py:21
  83.2 0.1 reshape.34
  83.3 0.3 multiply_convert_fusion
  83.6 0.2 copy.10
  83.8 9.2 %all_to_all.35 = bf16[2,128,1024]{1,2,0:T(8,128)(2,1)S(1)} all-to-all(bf16[2,128,1024]{1,2,0:T(8,128)(2,1)S(1)} %broadcast_in_dim.9), channel_id=1, replica_groups=mesh['xl'=2,'y'=4,'z'=8,'xh'=2,'core'=2] {'xh'}, dimensions={0} | all-to-all | bytes 1048576 | tf_op jit(solution)/shard_map/all_to_all | solution.py:21
  93.0 0.1 broadcast_in_dim.20
  93.1 4.6 %all_to_all.36 = bf16[2,2,128,1024]{2,3,1,0:T(8,128)(2,1)S(1)} all-to-all(bf16[2,2,128,1024]{2,3,1,0:T(8,128)(2,1)S(1)} %broadcast_in_dim.20), channel_id=1, replica_groups=mesh['xl'=2,'y'=4,'z'=8,'xh'=2,'core'=2] {'core'}, dimensions={0} | all-to-all | bytes 2097152 | tf_op jit(solution)/shard_map/all_to_all | solution.py:21
  97.7 0.1 copy.11
  97.8 19.2 %all_to_all.37 = bf16[8,128,512]{1,2,0:T(8,128)(2,1)S(1)} all-to-all(bf16[8,128,512]{1,2,0:T(8,128)(2,1)S(1)} %bitcast.21), channel_id=1, replica_groups=mesh['xl'=2,'y'=4,'z'=8,'xh'=2,'core'=2] {'xl','y'}, dimensions={0} | all-to-all | bytes 2097152 | tf_op jit(solution)/shard_map/all_to_all | solution.py:21
  117.0 0.3 broadcast_in_dim.21
  117.3 29.0 %all_to_all.38 = bf16[8,128,1024]{2,1,0:T(8,128)(2,1)S(1)} all-to-all(bf16[8,128,1024]{2,1,0:T(8,128)(2,1)S(1)} %broadcast_in_dim.21), channel_id=1, replica_groups=mesh['xl'=2,'y'=4,'z'=8,'xh'=2,'core'=2] {'xl','y'}, dimensions={0} | all-to-all | bytes 4194304 | tf_op jit(solution)/shard_map/all_to_all | solution.py:21
  146.3 1.2 bitcast_convert_fusion
  147.6 30.3 %all_to_all.39 = bf16[8,64,1024]{2,1,0:T(8,128)(2,1)S(1)} all-to-all(bf16[8,64,1024]{2,1,0:T(8,128)(2,1)S(1)} %bitcast.22), channel_id=1, replica_groups=mesh['xl'=2,'y'=4,'z'=8,'xh'=2,'core'=2] {'z'}, dimensions={0} | all-to-all | bytes 2097152 | tf_op jit(solution)/shard_map/all_to_all | solution.py:21
  177.9 0.9 convert_reduce_fusion
  (7 shorter events, 0.1 us)
Async XLA Ops:
  0.0 19.6 %copy-start.5 = (s32[128,1]{0,1:T(1,128)S(1)}, s32[128,1]{0,1:T(1,128)}, u32[]{:S(2)}) copy-start(s32[128,1]{0,1:T(1,128)} %param.9) | copy-start | bytes 1540
  0.0 19.8 %copy-start.2 = (bf16[128,512]{1,0:T(8,128)(2,1)S(1)}, bf16[128,512]{1,0:T(8,128)(2,1)}, u32[]{:S(2)}) copy-start(bf16[128,512]{1,0:T(8,128)(2,1)} %param.10) | copy-start | bytes 393220
  0.7 25.0 %collective-permute-start.3 = (f32[8,128]{1,0:T(8,128)S(1)}, f32[8,128]{1,0:T(8,128)S(1)}, u32[]{:S(2)}, u32[]{:S(2)}) collective-permute-start(f32[8,128]{1,0:T(8,128)S(1)} %pad_maximum_fusion), channel_id=1, source_target_pairs={{0,252},{4,0},{8,4},{12,8},{16,12},{20,16},{24,20},{28,24},{32,28}... | collective-permute-start | bytes 12296 | tf_op jit(solution)/shard_map/ppermute | solution.py:17
  9.7 16.1 %collective-permute-start.2 = (f32[8,128]{1,0:T(8,128)S(1)}, f32[8,128]{1,0:T(8,128)S(1)}, u32[]{:S(2)}, u32[]{:S(2)}) collective-permute-start(f32[8,128]{1,0:T(8,128)S(1)} %pad_maximum_fusion), channel_id=1, source_target_pairs={{0,4},{4,8},{8,12},{12,16},{16,20},{20,24},{24,28},{28,32},{32,36}... | collective-permute-start | bytes 12296 | tf_op jit(solution)/shard_map/ppermute | solution.py:17
  9.7 16.1 %copy-start.4 = (f32[4,128]{1,0:T(4,128)S(1)}, f32[4,128]{1,0:T(4,128)}, u32[]{:S(2)}) copy-start(f32[4,128]{1,0:T(4,128)} %param.7) | copy-start | bytes 6148
  9.7 16.7 %copy-start.3 = (f32[4,128]{1,0:T(4,128)S(1)}, f32[4,128]{1,0:T(4,128)}, u32[]{:S(2)}) copy-start(f32[4,128]{1,0:T(4,128)} %param.8) | copy-start | bytes 6148
  13.4 30.5 %collective-permute-start = (bf16[3,1024,128]{2,1,0:T(8,128)(2,1)}, bf16[3,1024,128]{2,1,0:T(8,128)(2,1)S(1)}, u32[]{:S(2)}, u32[]{:S(2)}) collective-permute-start(bf16[3,1024,128]{2,1,0:T(8,128)(2,1)} %get-tuple-element.7), channel_id=1, source_target_pairs={{0,4},{4,8},{8,12},{12,16},{16,20},{20,24},{24,28},{28,32},{32,36}... | collective-permute-start | bytes 2359304 | tf_op jit(solution)/shard_map/ppermute | solution.py:17
  13.4 30.5 %collective-permute-start.1 = (bf16[3,1024,128]{2,1,0:T(8,128)(2,1)}, bf16[3,1024,128]{2,1,0:T(8,128)(2,1)S(1)}, u32[]{:S(2)}, u32[]{:S(2)}) collective-permute-start(bf16[3,1024,128]{2,1,0:T(8,128)(2,1)} %get-tuple-element.8), channel_id=1, source_target_pairs={{0,252},{4,0},{8,4},{12,8},{16,12},{20,16},{24,20},{28,24},{32,28}... | collective-permute-start | bytes 2359304 | tf_op jit(solution)/shard_map/ppermute | solution.py:17
  21.1 22.1 %all-to-all-start = ((bf16[64,4,512]{2,1,0:T(4,128)(2,1)}), bf16[64,4,512]{2,1,0:T(4,128)(2,1)S(1)}, u32[]{:S(2)}, u32[]{:S(2)}) async-start(bf16[64,4,512]{2,1,0:T(4,128)(2,1)} %reshape.31), calls=%async_computation | async-start | bytes 524288 | tf_op jit(solution)/shard_map/all_to_all | solution.py:21
  43.9 0.9 copy-start
  44.8 0.9 copy-start.1
  55.0 11.4 %copy-start.6 = (bf16[128]{0:T(256)(128)(2,1)S(1)}, bf16[128]{0:T(256)(128)(2,1)}, u32[]{:S(2)}) copy-start(bf16[128]{0:T(256)(128)(2,1)} %param.11) | copy-start | bytes 772
  57.1 26.1 %all-to-all-start.1 = ((bf16[64,4,1024]{2,1,0:T(4,128)(2,1)}), bf16[64,4,1024]{2,1,0:T(4,128)(2,1)S(1)}, u32[]{:S(2)}, u32[]{:S(2)}) async-start(bf16[64,4,1024]{2,1,0:T(4,128)(2,1)} %reshape.33), calls=%async_computation.1 | async-start | bytes 1048576 | tf_op jit(solution)/shard_map/all_to_all | solution.py:21
